TPU v7x, 32 devices: a whole 2x2x4 slice. The times are simulated.
32 devices in a mesh: dom: 8 (over y, x, core), head: 4 (over z).
Axes of the slice: x: 2, y: 2, z: 4, core: 2. Of those that a mesh axis runs over, the one named last changes fastest.
Arguments:
- features: bfloat16 [25, 128, 4096], P(None, None, ('dom', 'head')), may hold values from -14 to 14
- positions: float32 [3, 4096], P(None, 'dom'), may hold values from 0 to 3
- penalty: float32 [16], replicated, may hold values from 0.01 to 0.5
- qk_weight: bfloat16 [128, 2048], replicated, may hold values from -0.5 to 0.5
- value_weight: bfloat16 [5, 128, 128], replicated, may hold values from -0.5 to 0.5
- output_weight: bfloat16 [5, 128, 128], replicated, may hold values from -0.5 to 0.5
- frames: float32 [64, 25, 25], replicated, may hold values from -3 to 3, as said below
- frame_index: int32 [64], P('dom'), may hold values from 0 to 63
- neighbours: int32 [64, 8], P('dom'), may hold values from 0 to 63, as said below
- counts: int32 [64], P('dom'), may hold values from 1 to 8
- cotangent: bfloat16 [25, 128, 4096], P(None, None, ('dom', 'head')), may hold values from -6 to 6
Outputs:
- updated: bfloat16 [25, 128, 4096], P(None, None, ('dom', 'head'))
- forces: float32 [3, 4096], P(None, ('dom', 'head'))
Inputs may be any that keep to these rules, and one draw needn't show every extreme that they name: `frames`: entries outside the diagonal blocks of components of one degree are zero. `neighbours`: row b holds 8 distinct blocks (b + o) mod 64 with |o| <= 4; the slots at and beyond counts[b] are padding.
All inputs are finite; a program needn't handle non-finite values.
Results may differ from a plain program's by a relative error of at most 0.0037.
The roundings to bfloat16 on the way count: a program that leaves them out, or rounds other values in their place, can miss the bound.
Values may be sent and summed in bfloat16 or wider, within the bound.
A program may use at most 64 MiB of HBM per device.

v0:
```python
import math
import jax
import jax.numpy as jnp
from jax import lax
from jax.sharding import PartitionSpec as P

COMP = 25
LDEG = 5
HEADS = 16
ALPHA = 64
BLOCK = 64
NBR = 8
REACH = 4
NFRAME = 64
NEG_FILL = -1e30


def extended(shard, sides, width):
    for axis, dim in sides:
        peers, length = (lax.axis_size(axis), shard.shape[dim])
        up = [(i, (i + 1) % peers) for i in range(peers)]
        down = [(j, i) for i, j in up]
        last = lax.slice_in_dim(shard, length - width, length, axis=dim)
        initial = lax.slice_in_dim(shard, 0, width, axis=dim)
        before = lax.ppermute(last, axis, up)
        after = lax.ppermute(initial, axis, down)
        shard = jnp.concatenate([before, shard, after], axis=dim)
    return shard


def from_behind(shard, axis, by):
    peers = lax.axis_size(axis)
    return lax.ppermute(shard, axis, [(i, (i + by) % peers) for i in range(peers)])


def degree_table():
    components = jnp.arange(COMP)
    degrees = jnp.sum(
        (components[:, None] >= (jnp.arange(1, LDEG) ** 2)[None, :]).astype(jnp.int32), axis=1
    )
    orders = components - degrees * degrees - degrees
    return (jnp.abs(orders) <= 2).astype(jnp.float32)


def projectors(frames):
    kept_mask = degree_table()
    return jnp.einsum("fji,j,fjk->fik", frames, kept_mask, frames, precision=lax.Precision.HIGHEST)


def mix_degrees(operand, weights, reverse):
    pieces = []
    for degree in range(weights.shape[0]):
        sliced = operand[degree * degree : (degree + 1) * (degree + 1)]
        if reverse:
            pieces.append(
                jnp.einsum(
                    "koa,co->kca", sliced, weights[degree], preferred_element_type=jnp.float32
                )
            )
        else:
            pieces.append(
                jnp.einsum(
                    "kca,co->koa", sliced, weights[degree], preferred_element_type=jnp.float32
                )
            )
    return jnp.concatenate(pieces, 0)


def pick_group(nblocks, heads_here):
    chosen = 1
    for candidate in range(1, nblocks + 1):
        if nblocks % candidate == 0 and candidate * BLOCK * heads_here <= 512:
            chosen = candidate
    return chosen


def block_meta(neighbours, counts, frame_index, projections, first_block, total_blocks):
    local_index = jnp.mod(neighbours - first_block + REACH, total_blocks)
    usable = jnp.arange(NBR)[None, :] < counts[:, None]
    onehot = (frame_index[:, None] == jnp.arange(NFRAME)[None, :]).astype(jnp.float32)
    matrices = jnp.dot(
        onehot, projections.reshape(NFRAME, COMP * COMP), precision=lax.Precision.HIGHEST
    )
    return (local_index, usable, matrices.reshape(-1, COMP, COMP))


def attend(
    queries,
    keys_ext,
    values_ext,
    grads,
    own_points,
    ext_points,
    penalty_here,
    local_index,
    usable,
    matrices,
):
    heads_here = penalty_here.shape[0]
    head_width = values_ext.shape[1] // heads_here
    query_blocks_count = queries.shape[1] // BLOCK
    ext_blocks = keys_ext.shape[1] // BLOCK
    query_blocks = queries.reshape(heads_here, ALPHA, query_blocks_count, BLOCK)
    key_blocks = keys_ext.reshape(heads_here, ALPHA, ext_blocks, BLOCK)
    value_blocks = values_ext.reshape(COMP, heads_here, head_width, ext_blocks, BLOCK)
    grad_blocks = grads.reshape(COMP, heads_here, head_width, query_blocks_count, BLOCK)
    own_blocks = own_points.reshape(3, query_blocks_count, BLOCK)
    ext_point_blocks = ext_points.reshape(3, ext_blocks, BLOCK)
    group_size = pick_group(query_blocks_count, heads_here)
    inverse_root = 1.0 / math.sqrt(ALPHA)
    block_range = jnp.arange(ext_blocks)

    def group_step(state_now, begin_at):
        attended_all, query_forces, ghost_forces = state_now
        slot_blocks = lax.dynamic_slice_in_dim(local_index, begin_at, group_size, 0)
        query_group = lax.dynamic_slice_in_dim(query_blocks, begin_at, group_size, 2)
        key_group = jnp.take(key_blocks, slot_blocks, axis=2)
        value_group = jnp.take(value_blocks, slot_blocks, axis=3)
        grad_group = lax.dynamic_slice_in_dim(grad_blocks, begin_at, group_size, 3)
        query_points = lax.dynamic_slice_in_dim(own_blocks, begin_at, group_size, 1)
        key_points = jnp.take(ext_point_blocks, slot_blocks, axis=1)
        live_slots = lax.dynamic_slice_in_dim(usable, begin_at, group_size, 0)
        group_mats = lax.dynamic_slice_in_dim(matrices, begin_at, group_size, 0)
        scores = (
            jnp.einsum(
                "hagi,hagsj->hgisj", query_group, key_group, preferred_element_type=jnp.float32
            )
            * inverse_root
        )
        separation = query_points[:, :, :, None, None] - key_points[:, :, None, :, :]
        distance = jnp.sum(separation * separation, axis=0)
        logits = scores - penalty_here[:, None, None, None, None] * distance[None]
        slot_mask = live_slots[None, :, None, :, None]
        logits = jnp.where(slot_mask, logits, NEG_FILL)
        peaks = jnp.max(logits, axis=(3, 4), keepdims=True)
        exponent = jnp.where(slot_mask, jnp.exp(logits - peaks), 0.0)
        attention = exponent / jnp.sum(exponent, axis=(3, 4), keepdims=True)
        rounded = attention.astype(jnp.bfloat16)
        aggregate = jnp.einsum(
            "hgisj,khdgsj->khdgi", rounded, value_group, preferred_element_type=jnp.float32
        )
        attended = jnp.einsum(
            "gkl,lhdgi->khdgi", group_mats, aggregate, precision=lax.Precision.HIGHEST
        ).astype(jnp.bfloat16)
        rotated = jnp.einsum(
            "glk,lhdgi->khdgi",
            group_mats,
            grad_group.astype(jnp.float32),
            precision=lax.Precision.HIGHEST,
        ).astype(jnp.bfloat16)
        weight_grads = jnp.einsum(
            "khdgi,khdgsj->hgisj", rotated, value_group, preferred_element_type=jnp.float32
        )
        logit_grads = attention * (
            weight_grads - jnp.sum(attention * weight_grads, axis=(3, 4), keepdims=True)
        )
        total = jnp.sum(2.0 * penalty_here[:, None, None, None, None] * logit_grads, axis=0)
        force_query = jnp.sum(total[None] * separation, axis=(3, 4))
        force_key = -jnp.sum(total[None] * separation, axis=2)
        onehot = (slot_blocks[:, :, None] == block_range[None, None, :]).astype(jnp.float32)
        ghost_forces = ghost_forces + jnp.einsum(
            "gse,cgsj->cej", onehot, force_key, precision=lax.Precision.HIGHEST
        )
        attended_all = lax.dynamic_update_slice_in_dim(attended_all, attended, begin_at, 3)
        query_forces = lax.dynamic_update_slice_in_dim(query_forces, force_query, begin_at, 1)
        return ((attended_all, query_forces, ghost_forces), None)

    initial = (
        jnp.zeros((COMP, heads_here, head_width, query_blocks_count, BLOCK), jnp.bfloat16),
        jnp.zeros((3, query_blocks_count, BLOCK), jnp.float32),
        jnp.zeros((3, ext_blocks, BLOCK), jnp.float32),
    )
    begins = jnp.arange(0, query_blocks_count, group_size)
    final_state, unused_out = lax.scan(group_step, initial, begins)
    attended_all, query_forces, ghost_forces = final_state
    return (
        attended_all.reshape(COMP, heads_here * head_width, query_blocks_count * BLOCK),
        query_forces.reshape(3, query_blocks_count * BLOCK),
        ghost_forces.reshape(3, ext_blocks * BLOCK),
    )


def on_device(
    features,
    positions,
    penalty,
    qk_weight,
    value_weight,
    output_weight,
    frames,
    frame_index,
    neighbours,
    counts,
    cotangent,
):
    atoms_here = features.shape[2]
    halo_width = REACH * BLOCK
    query_rows = HEADS * ALPHA
    projections = projectors(frames)
    grads = mix_degrees(cotangent, output_weight, True).astype(jnp.bfloat16)
    pos_ext = extended(positions, (("dom", 1),), halo_width)
    dom_atoms = positions.shape[1]
    dom_blocks = dom_atoms // BLOCK
    dom_count = lax.axis_size("dom")
    head_count = lax.axis_size("head")
    queries_keys = lax.dot_general(
        qk_weight, features[0], (((0,), (0,)), ((), ())), preferred_element_type=jnp.float32
    ).astype(jnp.bfloat16)
    values = mix_degrees(features, value_weight, False).astype(jnp.bfloat16)
    heads_here = HEADS // head_count
    paired = queries_keys.reshape(2, query_rows, atoms_here)
    paired_heads, values_heads, grads_heads = (
        lax.all_to_all(paired, "head", split_axis=1, concat_axis=2, tiled=True),
        lax.all_to_all(values, "head", split_axis=1, concat_axis=2, tiled=True),
        lax.all_to_all(grads, "head", split_axis=1, concat_axis=2, tiled=True),
    )
    packed = jnp.concatenate([paired_heads[1], values_heads.reshape(-1, dom_atoms)], 0)
    packed_ext = extended(packed, (("dom", 1),), halo_width)
    key_rows = heads_here * ALPHA
    penalty_here = lax.dynamic_slice_in_dim(
        penalty, lax.axis_index("head") * heads_here, heads_here
    )
    local_index, usable, matrices = block_meta(
        neighbours,
        counts,
        frame_index,
        projections,
        lax.axis_index("dom") * dom_blocks,
        dom_count * dom_blocks,
    )
    attended_all, force_query, force_ext = attend(
        paired_heads[0],
        packed_ext[:key_rows],
        packed_ext[key_rows:].reshape(COMP, -1, dom_atoms + 2 * halo_width),
        grads_heads,
        pos_ext[:, halo_width : halo_width + dom_atoms],
        pos_ext,
        penalty_here,
        local_index,
        usable,
        matrices,
    )
    attended_atoms = lax.all_to_all(attended_all, "head", split_axis=2, concat_axis=1, tiled=True)
    force_dom = force_query + force_ext[:, halo_width : halo_width + dom_atoms]
    for offset in (-1, 1):
        if offset < 0:
            rim_part = force_ext[:, :halo_width]
        else:
            rim_part = force_ext[:, halo_width + dom_atoms :]
        arrived = from_behind(rim_part, "dom", offset)
        if offset < 0:
            force_dom = force_dom.at[:, dom_atoms - halo_width :].add(arrived)
        else:
            force_dom = force_dom.at[:, :halo_width].add(arrived)
    forces = lax.psum_scatter(force_dom, "head", scatter_dimension=1, tiled=True)
    updated = (
        features.astype(jnp.float32) + mix_degrees(attended_atoms, output_weight, False)
    ).astype(jnp.bfloat16)
    return (updated, forces)


def solution(mesh):
    in_specs = (
        P(None, None, ("dom", "head")),
        P(None, "dom"),
        P(),
        P(),
        P(),
        P(),
        P(),
        P("dom"),
        P("dom", None),
        P("dom"),
        P(None, None, ("dom", "head")),
    )
    out_specs = (P(None, None, ("dom", "head")), P(None, ("dom", "head")))
    return jax.shard_map(
        on_device, mesh=mesh, in_specs=in_specs, out_specs=out_specs, check_vma=False
    )
```

profile of v0, /device:TPU:0, one launch (start us, length us, event | category | flops | bytes accessed | tf_op | source)
XLA Modules:
  0.0 372.3 jit_solution(10311147214418356075)
XLA Ops:
  10.7 6.3 %all-to-all-start = ((bf16[2,1024,128]{2,0,1:T(2,128)(2,1)}), bf16[2,1024,128]{2,0,1:T(2,128)(2,1)S(1)}, u32[]{:S(2)}, u32[]{:S(2)}) async-start(bf16[2,1024,128]{2,0,1:T(2,128)(2,1)} %copy.174), calls=%async_computation | async-start | bytes 1048576 | tf_op jit(solution)/shard_map/all_to_all | solution.py:213
  17.1 2.6 collective-permute-start.3
  21.1 1.5 copy.181
  23.3 8.2 %all-to-all-done = bf16[2,1024,128]{2,0,1:T(2,128)(2,1)S(1)} async-done(((bf16[2,1024,128]{2,0,1:T(2,128)(2,1)}), bf16[2,1024,128]{2,0,1:T(2,128)(2,1)S(1)}, u32[]{:S(2)}, u32[]{:S(2)}) %all-to-all-start) | async-done | bytes 524320 | tf_op jit(solution)/shard_map/all_to_all | solution.py:213
  31.5 4.3 %all-to-all-start.1 = ((bf16[25,128,128]{2,0,1:T(8,128)(2,1)}), bf16[25,128,128]{2,0,1:T(8,128)(2,1)}, u32[]{:S(2)}, u32[]{:S(2)}) async-start(bf16[25,128,128]{2,0,1:T(8,128)(2,1)} %copy.181), calls=%async_computation.1 | async-start | bytes 2097152 | tf_op jit(solution)/shard_map/all_to_all | solution.py:214
  36.1 1.5 copy.188
  38.8 1.8 copy.185
  40.6 2.4 convolution_bitcast_fusion.1
  43.0 18.1 %all-to-all-done.1 = bf16[25,128,128]{2,0,1:T(8,128)(2,1)} async-done(((bf16[25,128,128]{2,0,1:T(8,128)(2,1)}), bf16[25,128,128]{2,0,1:T(8,128)(2,1)}, u32[]{:S(2)}, u32[]{:S(2)}) %all-to-all-start.1) | async-done | bytes 819232 | tf_op jit(solution)/shard_map/all_to_all | solution.py:214
  61.1 3.5 all-to-all-start.2
  65.8 1.9 copy.182
  68.9 2.6 collective-permute-start.1
  71.7 1.5 copy.187
  74.3 1.6 fusion.105
  78.3 11.6 %all-to-all-done.2 = bf16[25,128,128]{2,0,1:T(8,128)(2,1)S(1)} async-done(((bf16[25,128,128]{2,0,1:T(8,128)(2,1)}), bf16[25,128,128]{2,0,1:T(8,128)(2,1)S(1)}, u32[]{:S(2)}, u32[]{:S(2)}) %all-to-all-start.2) | async-done | bytes 819232 | tf_op jit(solution)/shard_map/all_to_all | solution.py:215
  90.6 1.6 reshape.146
  95.8 3.4 reshape_reshape.3
  99.2 5.2 %copy.190 = bf16[25,4,8,16,64]{4,2,3,1,0:T(8,128)(2,1)} copy(bf16[25,4,8,16,64]{4,3,2,1,0:T(8,128)(2,1)} %reshape_reshape.3) | data formatting | bytes 3276800
  104.3 1.6 broadcast_in_dim.78.clone
  106.0 200.0 %while.17 = (s32[]{:T(128)}, bf16[25,4,8,8,64]{4,3,2,1,0:T(8,128)(2,1)}, f32[3,8,64]{2,1,0:T(8,128)S(1)}, f32[3,16,64]{2,1,0:T(8,128)S(1)}, s32[4]{0:T(128)S(1)}...) while((s32[]{:T(128)}, ...), condition=%wide.region_9.10_spmd.clone, body=%wide.region_1.9_spmd.clone.sunk | while | flops 315474432 | bytes 35243308 | solution.py:174
  115.2 1.9 constant_dynamic-slice_fusion.13
  118.1 5.3 %gather_fusion.2 = bf16[16,25,4,8,64]{4,3,2,1,0:T(8,128)(2,1)} fusion(bf16[25,4,8,16,64]{4,2,3,1,0:T(8,128)(2,1)} %get-tuple-element.472, s32[1024]{0:T(1024)S(1)} %pad_clamp_fusion.2), kind=kCustom, calls=%fused_computation.clone.clone.1 | custom fusion | bytes 3276864 | tf_op jit(solution)/shard_map/while/body/eval_jaxpr/jit(_take)/gather | solution.py:118
  123.4 4.2 %fusion.158 = (f32[4,2,64]{2,1,0:T(2,128)S(1)}, f32[4,2,64,8,64]{2,4,3,1,0:T(8,128)S(1)}, f32[4,2,64,8,64,1]{2,4,5,3,1,0:T(8,128)S(1)}) fusion(f32[4,2,64]{2,1,0:T(2,128)S(1)} %fusion.156, f32[4,2,64]{2,1,0:T(2,128)S(1)} %get-tuple-element.422, f32[2,64,8,64]{1,3,2,0:T(8,128)S(1)} %copy.287, f32[4]{0:T(128)S(1)} %get-tuple-element.476, ...), kind=kOutput, calls=%fused_computation.14.clone.1 | convolution fusion | flops 108035584 | bytes 5257264 | tf_op jit(solution)/shard_map/while/body/eval_jaxpr/khdgi,khdgsj->hgisj/dot_general | solution.py:151
  129.5 2.2 fusion.160
  133.2 21.0 %dynamic_update_slice.10 = bf16[25,4,8,8,64]{4,3,2,1,0:T(8,128)(2,1)} dynamic-update-slice(bf16[25,4,8,8,64]{4,3,2,1,0:T(8,128)(2,1)} %get-tuple-element.449, bf16[25,4,8,2,64]{4,3,2,1,0:T(2,128)(2,1)S(1)} %copy.289, s32[]{:T(128)} %constant.140.clone.1..sunk, s32[]{:T(128)} %constant.140.clone.1..sunk, s32[]{:T(128)} %constant.140.clone.1..sunk, s32[]{:T(128)S(6)} %select_n.111, ...) | dynamic-update-slice | bytes 409604 | tf_op jit(solution)/shard_map/while/body/eval_jaxpr/dynamic_update_slice | solution.py:164
  165.2 1.9 constant_dynamic-slice_fusion.13
  168.1 5.3 %gather_fusion.2 = bf16[16,25,4,8,64]{4,3,2,1,0:T(8,128)(2,1)} fusion(bf16[25,4,8,16,64]{4,2,3,1,0:T(8,128)(2,1)} %get-tuple-element.472, s32[1024]{0:T(1024)S(1)} %pad_clamp_fusion.2), kind=kCustom, calls=%fused_computation.clone.clone.1 | custom fusion | bytes 3276864 | tf_op jit(solution)/shard_map/while/body/eval_jaxpr/jit(_take)/gather | solution.py:118
  173.4 4.2 %fusion.158 = (f32[4,2,64]{2,1,0:T(2,128)S(1)}, f32[4,2,64,8,64]{2,4,3,1,0:T(8,128)S(1)}, f32[4,2,64,8,64,1]{2,4,5,3,1,0:T(8,128)S(1)}) fusion(f32[4,2,64]{2,1,0:T(2,128)S(1)} %fusion.156, f32[4,2,64]{2,1,0:T(2,128)S(1)} %get-tuple-element.422, f32[2,64,8,64]{1,3,2,0:T(8,128)S(1)} %copy.287, f32[4]{0:T(128)S(1)} %get-tuple-element.476, ...), kind=kOutput, calls=%fused_computation.14.clone.1 | convolution fusion | flops 108035584 | bytes 5257264 | tf_op jit(solution)/shard_map/while/body/eval_jaxpr/khdgi,khdgsj->hgisj/dot_general | solution.py:151
  179.5 2.2 fusion.160
  183.2 21.0 %dynamic_update_slice.10 = bf16[25,4,8,8,64]{4,3,2,1,0:T(8,128)(2,1)} dynamic-update-slice(bf16[25,4,8,8,64]{4,3,2,1,0:T(8,128)(2,1)} %get-tuple-element.449, bf16[25,4,8,2,64]{4,3,2,1,0:T(2,128)(2,1)S(1)} %copy.289, s32[]{:T(128)} %constant.140.clone.1..sunk, s32[]{:T(128)} %constant.140.clone.1..sunk, s32[]{:T(128)} %constant.140.clone.1..sunk, s32[]{:T(128)S(6)} %select_n.111, ...) | dynamic-update-slice | bytes 409604 | tf_op jit(solution)/shard_map/while/body/eval_jaxpr/dynamic_update_slice | solution.py:164
  215.2 1.9 constant_dynamic-slice_fusion.13
  218.1 5.3 %gather_fusion.2 = bf16[16,25,4,8,64]{4,3,2,1,0:T(8,128)(2,1)} fusion(bf16[25,4,8,16,64]{4,2,3,1,0:T(8,128)(2,1)} %get-tuple-element.472, s32[1024]{0:T(1024)S(1)} %pad_clamp_fusion.2), kind=kCustom, calls=%fused_computation.clone.clone.1 | custom fusion | bytes 3276864 | tf_op jit(solution)/shard_map/while/body/eval_jaxpr/jit(_take)/gather | solution.py:118
  223.4 4.2 %fusion.158 = (f32[4,2,64]{2,1,0:T(2,128)S(1)}, f32[4,2,64,8,64]{2,4,3,1,0:T(8,128)S(1)}, f32[4,2,64,8,64,1]{2,4,5,3,1,0:T(8,128)S(1)}) fusion(f32[4,2,64]{2,1,0:T(2,128)S(1)} %fusion.156, f32[4,2,64]{2,1,0:T(2,128)S(1)} %get-tuple-element.422, f32[2,64,8,64]{1,3,2,0:T(8,128)S(1)} %copy.287, f32[4]{0:T(128)S(1)} %get-tuple-element.476, ...), kind=kOutput, calls=%fused_computation.14.clone.1 | convolution fusion | flops 108035584 | bytes 5257264 | tf_op jit(solution)/shard_map/while/body/eval_jaxpr/khdgi,khdgsj->hgisj/dot_general | solution.py:151
  229.5 2.2 fusion.160
  233.2 21.0 %dynamic_update_slice.10 = bf16[25,4,8,8,64]{4,3,2,1,0:T(8,128)(2,1)} dynamic-update-slice(bf16[25,4,8,8,64]{4,3,2,1,0:T(8,128)(2,1)} %get-tuple-element.449, bf16[25,4,8,2,64]{4,3,2,1,0:T(2,128)(2,1)S(1)} %copy.289, s32[]{:T(128)} %constant.140.clone.1..sunk, s32[]{:T(128)} %constant.140.clone.1..sunk, s32[]{:T(128)} %constant.140.clone.1..sunk, s32[]{:T(128)S(6)} %select_n.111, ...) | dynamic-update-slice | bytes 409604 | tf_op jit(solution)/shard_map/while/body/eval_jaxpr/dynamic_update_slice | solution.py:164
  265.2 1.9 constant_dynamic-slice_fusion.13
  268.1 5.3 %gather_fusion.2 = bf16[16,25,4,8,64]{4,3,2,1,0:T(8,128)(2,1)} fusion(bf16[25,4,8,16,64]{4,2,3,1,0:T(8,128)(2,1)} %get-tuple-element.472, s32[1024]{0:T(1024)S(1)} %pad_clamp_fusion.2), kind=kCustom, calls=%fused_computation.clone.clone.1 | custom fusion | bytes 3276864 | tf_op jit(solution)/shard_map/while/body/eval_jaxpr/jit(_take)/gather | solution.py:118
  273.4 4.2 %fusion.158 = (f32[4,2,64]{2,1,0:T(2,128)S(1)}, f32[4,2,64,8,64]{2,4,3,1,0:T(8,128)S(1)}, f32[4,2,64,8,64,1]{2,4,5,3,1,0:T(8,128)S(1)}) fusion(f32[4,2,64]{2,1,0:T(2,128)S(1)} %fusion.156, f32[4,2,64]{2,1,0:T(2,128)S(1)} %get-tuple-element.422, f32[2,64,8,64]{1,3,2,0:T(8,128)S(1)} %copy.287, f32[4]{0:T(128)S(1)} %get-tuple-element.476, ...), kind=kOutput, calls=%fused_computation.14.clone.1 | convolution fusion | flops 108035584 | bytes 5257264 | tf_op jit(solution)/shard_map/while/body/eval_jaxpr/khdgi,khdgsj->hgisj/dot_general | solution.py:151
  279.5 2.2 fusion.160
  283.2 21.0 %dynamic_update_slice.10 = bf16[25,4,8,8,64]{4,3,2,1,0:T(8,128)(2,1)} dynamic-update-slice(bf16[25,4,8,8,64]{4,3,2,1,0:T(8,128)(2,1)} %get-tuple-element.449, bf16[25,4,8,2,64]{4,3,2,1,0:T(2,128)(2,1)S(1)} %copy.289, s32[]{:T(128)} %constant.140.clone.1..sunk, s32[]{:T(128)} %constant.140.clone.1..sunk, s32[]{:T(128)} %constant.140.clone.1..sunk, s32[]{:T(128)S(6)} %select_n.111, ...) | dynamic-update-slice | bytes 409604 | tf_op jit(solution)/shard_map/while/body/eval_jaxpr/dynamic_update_slice | solution.py:164
  306.0 3.0 reshape.147
  309.0 6.5 %copy.197 = bf16[25,32,512]{1,0,2:T(8,128)(2,1)} copy(bf16[25,32,512]{2,1,0:T(8,128)(2,1)S(1)} %reshape.147) | data formatting | bytes 1638400 | tf_op jit(solution)/shard_map/reshape | solution.py:177
  315.5 5.3 %reshape.212 = bf16[4,2,51200]{2,1,0:T(2,128)(2,1)} reshape(bf16[512,25,32]{2,1,0:T(8,128)(2,1)} %bitcast.289) | data formatting | bytes 1638400
  320.8 3.6 all-to-all-start.3
  327.8 2.6 collective-permute-done.5
  332.9 18.3 %reduce-scatter.4.cloned.1.call-done = f32[128,3]{1,0:T(8,128)} async-done(((f32[512,3]{1,0:T(8,128)}), f32[128,3]{1,0:T(8,128)}) %reduce-scatter.4.cloned.1.call-update) | async-done | bytes 1552
  352.7 4.1 %reshape.213 = bf16[512,25,32]{2,1,0:T(8,128)(2,1)} reshape(bf16[4,2,51200]{2,1,0:T(2,128)(2,1)S(1)} %all-to-all-done.3) | data formatting | bytes 1638400
  356.8 5.2 %copy.220 = bf16[25,32,4,128]{3,2,1,0:T(4,128)(2,1)S(1)} copy(bf16[25,32,4,128]{1,0,3,2:T(8,128)(2,1)} %bitcast.290) | data formatting | bytes 1638400 | tf_op jit(solution)/shard_map/all_to_all | solution.py:243
  (243 shorter events, 80.6 us)
Async XLA Ops:
  7.2 1.1 copy-start
  7.2 12.6 %copy-start.5 = (bf16[25,128,128]{2,1,0:T(8,128)(2,1)S(1)}, bf16[25,128,128]{2,1,0:T(8,128)(2,1)}, u32[]{:S(2)}) copy-start(bf16[25,128,128]{2,1,0:T(8,128)(2,1)} %param.17) | copy-start | bytes 2457604
  7.2 9.8 %copy-start.12 = (f32[3,512]{1,0:T(4,128)S(1)}, f32[3,512]{1,0:T(4,128)}, u32[]{:S(2)}) copy-start(f32[3,512]{1,0:T(4,128)} %param.18) | copy-start | bytes 18436
  7.2 12.5 %copy-start.11 = (bf16[5,128,128]{2,1,0:T(8,128)(2,1)S(1)}, bf16[5,128,128]{2,1,0:T(8,128)(2,1)}, u32[]{:S(2)}) copy-start(bf16[5,128,128]{2,1,0:T(8,128)(2,1)} %param.21) | copy-start | bytes 491524
  9.3 11.7 %copy-start.8 = (bf16[25,128,128]{2,1,0:T(8,128)(2,1)S(1)}, bf16[25,128,128]{2,1,0:T(8,128)(2,1)}, u32[]{:S(2)}) copy-start(bf16[25,128,128]{2,1,0:T(8,128)(2,1)} %param.27) | copy-start | bytes 2457604
  9.3 11.7 %copy-start.9 = (bf16[5,128,128]{2,1,0:T(8,128)(2,1)S(1)}, bf16[5,128,128]{2,1,0:T(8,128)(2,1)}, u32[]{:S(2)}) copy-start(bf16[5,128,128]{2,1,0:T(8,128)(2,1)} %param.22) | copy-start | bytes 491524
  10.7 20.8 %all-to-all-start = ((bf16[2,1024,128]{2,0,1:T(2,128)(2,1)}), bf16[2,1024,128]{2,0,1:T(2,128)(2,1)S(1)}, u32[]{:S(2)}, u32[]{:S(2)}) async-start(bf16[2,1024,128]{2,0,1:T(2,128)(2,1)} %copy.174), calls=%async_computation | async-start | bytes 1048576 | tf_op jit(solution)/shard_map/all_to_all | solution.py:213
  17.0 58.9 %collective-permute-start.2 = (f32[3,256]{1,0:T(4,128)S(1)}, f32[3,256]{1,0:T(4,128)S(1)}, u32[]{:S(2)}, u32[]{:S(2)}) collective-permute-start(f32[3,256]{1,0:T(4,128)S(1)} %get-tuple-element.313), channel_id=1, source_target_pairs={{0,4},{4,8},{8,12},{12,16},{16,20},{20,24},{24,28},{28,0},{1,5},{5... | collective-permute-start | bytes 9224 | tf_op jit(solution)/shard_map/ppermute | solution.py:25
  17.1 58.9 %collective-permute-start.3 = (f32[3,256]{1,0:T(4,128)S(1)}, f32[3,256]{1,0:T(4,128)S(1)}, u32[]{:S(2)}, u32[]{:S(2)}) collective-permute-start(f32[3,256]{1,0:T(4,128)S(1)} %get-tuple-element.314), channel_id=1, source_target_pairs={{4,0},{8,4},{12,8},{16,12},{20,16},{24,20},{28,24},{0,28},{5,1},{9... | collective-permute-start | bytes 9224 | tf_op jit(solution)/shard_map/ppermute | solution.py:26
  23.3 14.3 %copy-start.7 = (f32[64,25,25]{0,2,1:T(8,128)S(1)}, f32[64,25,25]{0,2,1:T(8,128)}, u32[]{:S(2)}) copy-start(f32[64,25,25]{0,2,1:T(8,128)} %param.23) | copy-start | bytes 480004
  31.5 29.6 %all-to-all-start.1 = ((bf16[25,128,128]{2,0,1:T(8,128)(2,1)}), bf16[25,128,128]{2,0,1:T(8,128)(2,1)}, u32[]{:S(2)}, u32[]{:S(2)}) async-start(bf16[25,128,128]{2,0,1:T(8,128)(2,1)} %copy.181), calls=%async_computation.1 | async-start | bytes 2097152 | tf_op jit(solution)/shard_map/all_to_all | solution.py:214
  40.6 24.0 %copy-start.13 = (s32[8,8]{1,0:T(8,128)S(1)}, s32[8,8]{1,0:T(8,128)}, u32[]{:S(2)}) copy-start(s32[8,8]{1,0:T(8,128)} %param.25) | copy-start | bytes 772
  61.1 28.8 %all-to-all-start.2 = ((bf16[25,128,128]{2,0,1:T(8,128)(2,1)}), bf16[25,128,128]{2,0,1:T(8,128)(2,1)S(1)}, u32[]{:S(2)}, u32[]{:S(2)}) async-start(bf16[25,128,128]{2,0,1:T(8,128)(2,1)} %copy.188), calls=%async_computation.2 | async-start | bytes 2097152 | tf_op jit(solution)/shard_map/all_to_all | solution.py:215
  67.7 3.9 %copy-start.15 = (s32[8]{0:T(128)S(1)}, s32[8]{0:T(128)}, u32[]{:S(2)}) copy-start(s32[8]{0:T(128)} %param.26) | copy-start | bytes 100
  67.8 6.4 %copy-start.14 = (s32[8]{0:T(128)S(1)}, s32[8]{0:T(128)}, u32[]{:S(2)}) copy-start(s32[8]{0:T(128)} %param.24) | copy-start | bytes 100
  68.9 7.0 %copy-start.16 = (f32[16]{0:T(128)S(1)}, f32[16]{0:T(128)}, u32[]{:S(2)}) copy-start(f32[16]{0:T(128)} %param.19) | copy-start | bytes 196
  68.9 23.3 %collective-permute-start = (bf16[1056,256]{1,0:T(8,128)(2,1)}, bf16[1056,256]{1,0:T(8,128)(2,1)}, u32[]{:S(2)}, u32[]{:S(2)}) collective-permute-start(bf16[1056,256]{1,0:T(8,128)(2,1)} %get-tuple-element.307), channel_id=1, source_target_pairs={{0,4},{4,8},{8,12},{12,16},{16,20},{20,24},{24,28},{28,0},{1,5},{5... | collective-permute-start | bytes 1622024 | tf_op jit(solution)/shard_map/ppermute | solution.py:25
  68.9 23.3 %collective-permute-start.1 = (bf16[1056,256]{1,0:T(8,128)(2,1)}, bf16[1056,256]{1,0:T(8,128)(2,1)}, u32[]{:S(2)}, u32[]{:S(2)}) collective-permute-start(bf16[1056,256]{1,0:T(8,128)(2,1)} %get-tuple-element.308), channel_id=1, source_target_pairs={{4,0},{8,4},{12,8},{16,12},{20,16},{24,20},{28,24},{0,28},{5,1},{9... | collective-permute-start | bytes 1622024 | tf_op jit(solution)/shard_map/ppermute | solution.py:26
  106.0 4.9 %copy-start.3 = (bf16[4,64,16,64]{3,1,2,0:T(8,128)(2,1)}, bf16[4,64,16,64]{3,1,2,0:T(8,128)(2,1)S(1)}, u32[]{:S(2)}) copy-start(bf16[4,64,16,64]{3,1,2,0:T(8,128)(2,1)S(1)} %get-tuple-element.475) | copy-start | bytes 1572868 | tf_op jit(solution)/shard_map/while
  127.6 1.9 copy-start.2
  132.7 23.2 %copy-start.4 = (bf16[4,64,16,64]{3,1,2,0:T(8,128)(2,1)S(1)}, bf16[4,64,16,64]{3,1,2,0:T(8,128)(2,1)}, u32[]{:S(2)}) copy-start(bf16[4,64,16,64]{3,1,2,0:T(8,128)(2,1)} %copy-done.3) | copy-start | bytes 1572868 | tf_op jit(solution)/shard_map/while
  156.0 4.9 %copy-start.3 = (bf16[4,64,16,64]{3,1,2,0:T(8,128)(2,1)}, bf16[4,64,16,64]{3,1,2,0:T(8,128)(2,1)S(1)}, u32[]{:S(2)}) copy-start(bf16[4,64,16,64]{3,1,2,0:T(8,128)(2,1)S(1)} %get-tuple-element.475) | copy-start | bytes 1572868 | tf_op jit(solution)/shard_map/while
  177.6 1.9 copy-start.2
  182.7 23.2 %copy-start.4 = (bf16[4,64,16,64]{3,1,2,0:T(8,128)(2,1)S(1)}, bf16[4,64,16,64]{3,1,2,0:T(8,128)(2,1)}, u32[]{:S(2)}) copy-start(bf16[4,64,16,64]{3,1,2,0:T(8,128)(2,1)} %copy-done.3) | copy-start | bytes 1572868 | tf_op jit(solution)/shard_map/while
  206.0 4.9 %copy-start.3 = (bf16[4,64,16,64]{3,1,2,0:T(8,128)(2,1)}, bf16[4,64,16,64]{3,1,2,0:T(8,128)(2,1)S(1)}, u32[]{:S(2)}) copy-start(bf16[4,64,16,64]{3,1,2,0:T(8,128)(2,1)S(1)} %get-tuple-element.475) | copy-start | bytes 1572868 | tf_op jit(solution)/shard_map/while
  227.6 1.9 copy-start.2
  232.7 23.2 %copy-start.4 = (bf16[4,64,16,64]{3,1,2,0:T(8,128)(2,1)S(1)}, bf16[4,64,16,64]{3,1,2,0:T(8,128)(2,1)}, u32[]{:S(2)}) copy-start(bf16[4,64,16,64]{3,1,2,0:T(8,128)(2,1)} %copy-done.3) | copy-start | bytes 1572868 | tf_op jit(solution)/shard_map/while
  256.0 4.9 %copy-start.3 = (bf16[4,64,16,64]{3,1,2,0:T(8,128)(2,1)}, bf16[4,64,16,64]{3,1,2,0:T(8,128)(2,1)S(1)}, u32[]{:S(2)}) copy-start(bf16[4,64,16,64]{3,1,2,0:T(8,128)(2,1)S(1)} %get-tuple-element.475) | copy-start | bytes 1572868 | tf_op jit(solution)/shard_map/while
  277.6 1.9 copy-start.2
  282.8 23.2 %copy-start.4 = (bf16[4,64,16,64]{3,1,2,0:T(8,128)(2,1)S(1)}, bf16[4,64,16,64]{3,1,2,0:T(8,128)(2,1)}, u32[]{:S(2)}) copy-start(bf16[4,64,16,64]{3,1,2,0:T(8,128)(2,1)} %copy-done.3) | copy-start | bytes 1572868 | tf_op jit(solution)/shard_map/while
  320.8 11.1 %copy-start.6 = (bf16[25,128,128]{2,1,0:T(8,128)(2,1)S(1)}, bf16[25,128,128]{2,1,0:T(8,128)(2,1)}, u32[]{:S(2)}) copy-start(bf16[25,128,128]{2,1,0:T(8,128)(2,1)} %param.17) | copy-start | bytes 2457604
  320.8 31.9 %all-to-all-start.3 = ((bf16[4,2,51200]{2,1,0:T(2,128)(2,1)}), bf16[4,2,51200]{2,1,0:T(2,128)(2,1)S(1)}, u32[]{:S(2)}, u32[]{:S(2)}) async-start(bf16[4,2,51200]{2,1,0:T(2,128)(2,1)} %reshape.212), calls=%async_computation.3 | async-start | bytes 1638400 | tf_op jit(solution)/shard_map/all_to_all | solution.py:243
  324.4 26.8 %reduce-scatter.4.cloned.1.call-start = ((), (), s32[]{:S(2)}) async-start(), calls=%async_computation.5 | async-start | bytes 327680
  325.3 2.5 collective-permute-start.4
  326.4 3.9 %collective-permute-start.5 = (f32[3,256]{1,0:T(4,128)S(1)}, f32[3,256]{1,0:T(4,128)S(1)}, u32[]{:S(2)}, u32[]{:S(2)}) collective-permute-start(f32[3,256]{1,0:T(4,128)S(1)} %get-tuple-element.311), channel_id=1, source_target_pairs={{0,4},{4,8},{8,12},{12,16},{16,20},{20,24},{24,28},{28,0},{1,5},{5... | collective-permute-start | bytes 9224 | tf_op jit(solution)/shard_map/ppermute | solution.py:33
  356.8 5.6 %copy-start.10 = (bf16[5,128,128]{2,1,0:T(8,128)(2,1)S(1)}, bf16[5,128,128]{2,1,0:T(8,128)(2,1)}, u32[]{:S(2)}) copy-start(bf16[5,128,128]{2,1,0:T(8,128)(2,1)} %param.22) | copy-start | bytes 491524
  363.5 2.0 copy-start.1
Sparse Core Ops, SparseCore 0:
  332.0 19.1 reduce-scatter.3
where the time goes:
time: 375 us; the launch traced here: 372 us
  local copies, waits for them, and re-layouts  201 us (54%)
  waiting for transfers between devices  60.1 us (16%)
  matrix products  45.4 us (12%)
  starting transfers between devices  24.3 us (6%)
  other arithmetic  18.4 us (5%)
  between operations  14.6 us (4%)
  loops' own time  8.68 us (2%)
    dynamic_update_slice x8, local copies, waits for them, and re-layouts, group_step(): lax.dynamic_update_slice_in_dim(attended_all, attended, begin_at, 3)  85.9 us
    unnamed x39, local copies, waits for them, and re-layouts  21.9 us
    gather x4, local copies, waits for them, and re-layouts, group_step(): value_group = jnp.take(value_blocks, slot_blocks, axis=3)  21 us
    unnamed x2, waiting for transfers between devices  18.3 us
    all_to_all x1, waiting for transfers between devices, on_device(): lax.all_to_all(values, 'head', split_axis=1, concat_axis=2, tiled=True)  18.1 us
    dot_general x4, matrix products, group_step(): jnp.einsum('khdgi,khdgsj->hgisj', rotated, value_group, preferred_element...  16.7 us
    all_to_all x1, waiting for transfers between devices, on_device(): lax.all_to_all(grads, 'head', split_axis=1, concat_axis=2, tiled=True)  11.6 us
    reshape x2, local copies, waits for them, and re-layouts, attend(): attended_all.reshape(COMP, heads_here * head_width, query_blocks_count *...  9.53 us
  transfers between devices with their start and end apart: 11, of which 6 were waited for; matrix products, arithmetic and copies ran while one was open for 8% of the time, Pallas kernels for 0%

commit v1 on v0

--- a/solution.py
+++ b/solution.py
@@ -13,6 +13,33 @@
 REACH = 4
 NFRAME = 64
 NEG_FILL = -1e30
+
+
+def step_on_loops(u, d_out, panel):
+    state_next, opened = (u.shape[:d_out], u.shape[d_out + 1 :])
+    return jnp.moveaxis(u.reshape(*state_next, panel, -1, *opened), d_out, 0)
+
+
+def time_copies(a0, dim_k):
+    a0 = jnp.moveaxis(a0, 0, dim_k)
+    mixed_arr = a0.shape
+    return a0.reshape(
+        *mixed_arr[:dim_k], mixed_arr[dim_k] * mixed_arr[dim_k + 1], *mixed_arr[dim_k + 2 :]
+    )
+
+
+def spread_record(xs, chip_axis, x_part, v0=2):
+    inter, plain = (lax.axis_size(chip_axis), lax.axis_index(chip_axis))
+    low = step_on_loops(xs, x_part, inter)
+    met_up = low
+    for tick in range(1, inter):
+        local_next, y2 = ((plain + tick) % inter, (plain - tick) % inter)
+        parts_out = lax.dynamic_index_in_dim(low, local_next, 0)
+        u_next = lax.ppermute(
+            parts_out, chip_axis, [(dd, (dd + tick) % inter) for dd in range(inter)]
+        )
+        met_up = lax.dynamic_update_slice_in_dim(met_up, u_next, y2, axis=0)
+    return time_copies(met_up, v0)
 
 
 def extended(shard, sides, width):
@@ -211,7 +238,7 @@
     paired = queries_keys.reshape(2, query_rows, atoms_here)
     paired_heads, values_heads, grads_heads = (
         lax.all_to_all(paired, "head", split_axis=1, concat_axis=2, tiled=True),
-        lax.all_to_all(values, "head", split_axis=1, concat_axis=2, tiled=True),
+        spread_record(values, "head", x_part=1),
         lax.all_to_all(grads, "head", split_axis=1, concat_axis=2, tiled=True),
     )
     packed = jnp.concatenate([paired_heads[1], values_heads.reshape(-1, dom_atoms)], 0)

time: 375 us -> 409 us (1.091)
  local copies, waits for them, and re-layouts: 201 us -> 229 us
  waiting for transfers between devices: 60.1 us -> 51 us
  matrix products: 45.4 us -> 54.3 us
    dynamic_update_slice x0 -> x3, local copies, waits for them, and re-layouts: none -> 30.5 us  [spread_record(): met_up = lax.dynamic_update_slice_in_dim(met_up, u_next, y2, axis=0)]
    all_to_all x1 -> x0, waiting for transfers between devices: 18.1 us -> none  [on_device(): lax.all_to_all(values, 'head', split_axis=1, concat_axis=2, tiled=True)]
    all_to_all x1, waiting for transfers between devices: 8.21 us -> 24.3 us  [on_device(): lax.all_to_all(paired, 'head', split_axis=1, concat_axis=2, tiled=True)]
    all_to_all x1, waiting for transfers between devices: 11.6 us -> 0.01 us  [on_device(): lax.all_to_all(grads, 'head', split_axis=1, concat_axis=2, tiled=True)]
    ppermute x0 -> x3, starting transfers between devices: none -> 6.99 us  [spread_record(): lax.ppermute(parts_out, chip_axis, [(dd, (dd + tick) % inter) for dd in r...]
    dot_general x5, matrix products: 1 us -> 5.48 us  [mix_degrees(): jnp.einsum('koa,co->kca', sliced, weights[degree], preferred_element_type...]
    dot_general x10, matrix products: 2.36 us -> 6.78 us  [mix_degrees(): jnp.einsum('kca,co->koa', sliced, weights[degree], preferred_element_type...]
    all_to_all x1 -> x0, starting transfers between devices: 4.26 us -> none  [on_device(): lax.all_to_all(values, 'head', split_axis=1, concat_axis=2, tiled=True)]
  transfers between devices with their start and end apart: 11 -> 13, of which waited for: 6 -> 5; matrix products, arithmetic and copies ran while one was open for 8% -> 15% of each run, Pallas kernels for 0% -> 0%
where the time goes in v1:
time: 409 us; the launch traced here: 403 us
  local copies, waits for them, and re-layouts  229 us (56%)
  matrix products  54.3 us (13%)
  waiting for transfers between devices  51 us (12%)
  starting transfers between devices  27.7 us (7%)
  other arithmetic  18.4 us (4%)
  between operations  14.7 us (4%)
  loops' own time  8.68 us (2%)
    dynamic_update_slice x8, local copies, waits for them, and re-layouts, group_step(): lax.dynamic_update_slice_in_dim(attended_all, attended, begin_at, 3)  85.8 us
    dynamic_update_slice x3, local copies, waits for them, and re-layouts, spread_record(): met_up = lax.dynamic_update_slice_in_dim(met_up, u_next, y2, axis=0)  30.5 us
    all_to_all x1, waiting for transfers between devices, on_device(): lax.all_to_all(paired, 'head', split_axis=1, concat_axis=2, tiled=True)  24.3 us
    unnamed x37, local copies, waits for them, and re-layouts  21.2 us
    gather x4, local copies, waits for them, and re-layouts, group_step(): value_group = jnp.take(value_blocks, slot_blocks, axis=3)  21 us
    unnamed x2, waiting for transfers between devices  19.1 us
    dot_general x4, matrix products, group_step(): jnp.einsum('khdgi,khdgsj->hgisj', rotated, value_group, preferred_element...  16.7 us
    reshape x2, local copies, waits for them, and re-layouts, attend(): attended_all.reshape(COMP, heads_here * head_width, query_blocks_count *...  9.54 us
  transfers between devices with their start and end apart: 13, of which 5 were waited for; matrix products, arithmetic and copies ran while one was open for 15% of the time, Pallas kernels for 0%

profile of v1, /device:TPU:0, one launch (start us, length us, event | category | flops | bytes accessed | tf_op | source)
XLA Modules:
  0.0 403.4 jit_solution(14868410739931379946)
XLA Ops:
  14.3 2.4 dynamic-slice_bitcast_fusion
  16.8 3.0 collective-permute-start
  19.8 2.6 collective-permute-start.1
  26.2 3.5 all-to-all-start
  29.8 2.6 collective-permute-start.6
  40.6 1.8 copy.209
  42.5 2.4 convolution_bitcast_fusion.1
  44.9 24.3 %all-to-all-done = bf16[2,1024,128]{2,0,1:T(2,128)(2,1)S(1)} async-done(((bf16[2,1024,128]{2,0,1:T(2,128)(2,1)}), bf16[2,1024,128]{2,0,1:T(2,128)(2,1)S(1)}, u32[]{:S(2)}, u32[]{:S(2)}) %all-to-all-start) | async-done | bytes 524320 | tf_op jit(solution)/shard_map/all_to_all | solution.py:240
  69.2 4.3 %all-to-all-start.1 = ((bf16[25,128,128]{2,0,1:T(8,128)(2,1)}), bf16[25,128,128]{2,0,1:T(8,128)(2,1)}, u32[]{:S(2)}, u32[]{:S(2)}) async-start(bf16[25,128,128]{2,0,1:T(8,128)(2,1)} %copy.212), calls=%async_computation.1 | async-start | bytes 2097152 | tf_op jit(solution)/shard_map/all_to_all | solution.py:242
  73.5 10.2 %dynamic_update_slice.15 = bf16[4,25,32,128]{3,0,2,1:T(4,128)(2,1)S(1)} dynamic-update-slice(bf16[4,25,32,128]{3,0,2,1:T(4,128)(2,1)S(1)} %bitcast.298, bf16[1,25,32,128]{3,0,2,1:T(2,128)(2,1)} %collective-permute-done, s32[]{:T(128)S(6)} %select_n.101, s32[]{:T(128)} %constant.183.clone.1, s32[]{:T(128)} %constant.183.clone.1, s32[]{:T(128)} %constant.183.clone.1) | dynamic-update-slice | bytes 409604 | tf_op jit(solution)/shard_map/dynamic_update_slice | solution.py:41
  83.7 10.2 %dynamic_update_slice.16 = bf16[4,25,32,128]{3,0,2,1:T(4,128)(2,1)S(1)} dynamic-update-slice(bf16[4,25,32,128]{3,0,2,1:T(4,128)(2,1)S(1)} %dynamic_update_slice.15, bf16[1,25,32,128]{3,0,2,1:T(2,128)(2,1)} %collective-permute-done.1, s32[]{:T(128)S(6)} %select_n.105, s32[]{:T(128)} %constant.183.clone.1, s32[]{:T(128)} %constant.183.clone.1, s32[]{:T(128)} %constant.183.clone.1) | dynamic-update-slice | bytes 409604 | tf_op jit(solution)/shard_map/dynamic_update_slice | solution.py:41
  93.9 10.2 %dynamic_update_slice.17 = bf16[4,25,32,128]{3,0,2,1:T(4,128)(2,1)S(1)} dynamic-update-slice(bf16[4,25,32,128]{3,0,2,1:T(4,128)(2,1)S(1)} %dynamic_update_slice.16, bf16[1,25,32,128]{3,0,2,1:T(2,128)(2,1)} %collective-permute-done.2, s32[]{:T(128)S(6)} %select_n.109, s32[]{:T(128)} %constant.183.clone.1, s32[]{:T(128)} %constant.183.clone.1, s32[]{:T(128)} %constant.183.clone.1) | dynamic-update-slice | bytes 409604 | tf_op jit(solution)/shard_map/dynamic_update_slice | solution.py:41
  105.7 2.6 collective-permute-start.4
  112.4 1.9 copy.293
  115.9 3.7 collective-permute-done.3
  123.2 3.4 reshape_reshape.7
  126.6 5.2 %copy.214 = bf16[25,4,8,16,64]{4,2,3,1,0:T(8,128)(2,1)} copy(bf16[25,4,8,16,64]{4,3,2,1,0:T(8,128)(2,1)} %reshape_reshape.7) | data formatting | bytes 3276800
  131.8 1.7 broadcast_in_dim.78.clone
  133.4 200.0 %while.17 = (s32[]{:T(128)}, bf16[25,4,8,8,64]{4,3,2,1,0:T(8,128)(2,1)}, f32[3,8,64]{2,1,0:T(8,128)S(1)}, f32[3,16,64]{2,1,0:T(8,128)S(1)}, s32[4]{0:T(128)S(1)}...) while((s32[]{:T(128)}, ...), condition=%wide.region_9.10_spmd.clone, body=%wide.region_1.9_spmd.clone.sunk | while | flops 315474432 | bytes 35243308 | solution.py:201
  142.7 1.9 constant_dynamic-slice_fusion.13
  145.6 5.3 %gather_fusion.2 = bf16[16,25,4,8,64]{4,3,2,1,0:T(8,128)(2,1)} fusion(bf16[25,4,8,16,64]{4,2,3,1,0:T(8,128)(2,1)} %get-tuple-element.475, s32[1024]{0:T(1024)S(1)} %pad_clamp_fusion.2), kind=kCustom, calls=%fused_computation.clone.clone.1 | custom fusion | bytes 3276864 | tf_op jit(solution)/shard_map/while/body/eval_jaxpr/jit(_take)/gather | solution.py:145
  150.8 4.2 %fusion.148 = (f32[4,2,64]{2,1,0:T(2,128)S(1)}, f32[4,2,64,8,64]{2,4,3,1,0:T(8,128)S(1)}, f32[4,2,64,8,64,1]{2,4,5,3,1,0:T(8,128)S(1)}) fusion(f32[4,2,64]{2,1,0:T(2,128)S(1)} %fusion.146, f32[4,2,64]{2,1,0:T(2,128)S(1)} %get-tuple-element.425, f32[2,64,8,64]{1,3,2,0:T(8,128)S(1)} %copy.316, f32[4]{0:T(128)S(1)} %get-tuple-element.479, ...), kind=kOutput, calls=%fused_computation.14.clone.1 | convolution fusion | flops 108035584 | bytes 5257264 | tf_op jit(solution)/shard_map/while/body/eval_jaxpr/khdgi,khdgsj->hgisj/dot_general | solution.py:178
  156.9 2.2 fusion.150
  160.6 21.0 %dynamic_update_slice.22 = bf16[25,4,8,8,64]{4,3,2,1,0:T(8,128)(2,1)} dynamic-update-slice(bf16[25,4,8,8,64]{4,3,2,1,0:T(8,128)(2,1)} %get-tuple-element.452, bf16[25,4,8,2,64]{4,3,2,1,0:T(2,128)(2,1)S(1)} %copy.318, s32[]{:T(128)} %constant.183.clone.1..sunk, s32[]{:T(128)} %constant.183.clone.1..sunk, s32[]{:T(128)} %constant.183.clone.1..sunk, s32[]{:T(128)S(6)} %select_n.168, ...) | dynamic-update-slice | bytes 409604 | tf_op jit(solution)/shard_map/while/body/eval_jaxpr/dynamic_update_slice | solution.py:191
  192.7 1.9 constant_dynamic-slice_fusion.13
  195.6 5.3 %gather_fusion.2 = bf16[16,25,4,8,64]{4,3,2,1,0:T(8,128)(2,1)} fusion(bf16[25,4,8,16,64]{4,2,3,1,0:T(8,128)(2,1)} %get-tuple-element.475, s32[1024]{0:T(1024)S(1)} %pad_clamp_fusion.2), kind=kCustom, calls=%fused_computation.clone.clone.1 | custom fusion | bytes 3276864 | tf_op jit(solution)/shard_map/while/body/eval_jaxpr/jit(_take)/gather | solution.py:145
  200.8 4.2 %fusion.148 = (f32[4,2,64]{2,1,0:T(2,128)S(1)}, f32[4,2,64,8,64]{2,4,3,1,0:T(8,128)S(1)}, f32[4,2,64,8,64,1]{2,4,5,3,1,0:T(8,128)S(1)}) fusion(f32[4,2,64]{2,1,0:T(2,128)S(1)} %fusion.146, f32[4,2,64]{2,1,0:T(2,128)S(1)} %get-tuple-element.425, f32[2,64,8,64]{1,3,2,0:T(8,128)S(1)} %copy.316, f32[4]{0:T(128)S(1)} %get-tuple-element.479, ...), kind=kOutput, calls=%fused_computation.14.clone.1 | convolution fusion | flops 108035584 | bytes 5257264 | tf_op jit(solution)/shard_map/while/body/eval_jaxpr/khdgi,khdgsj->hgisj/dot_general | solution.py:178
  206.9 2.2 fusion.150
  210.6 21.0 %dynamic_update_slice.22 = bf16[25,4,8,8,64]{4,3,2,1,0:T(8,128)(2,1)} dynamic-update-slice(bf16[25,4,8,8,64]{4,3,2,1,0:T(8,128)(2,1)} %get-tuple-element.452, bf16[25,4,8,2,64]{4,3,2,1,0:T(2,128)(2,1)S(1)} %copy.318, s32[]{:T(128)} %constant.183.clone.1..sunk, s32[]{:T(128)} %constant.183.clone.1..sunk, s32[]{:T(128)} %constant.183.clone.1..sunk, s32[]{:T(128)S(6)} %select_n.168, ...) | dynamic-update-slice | bytes 409604 | tf_op jit(solution)/shard_map/while/body/eval_jaxpr/dynamic_update_slice | solution.py:191
  242.7 1.9 constant_dynamic-slice_fusion.13
  245.6 5.3 %gather_fusion.2 = bf16[16,25,4,8,64]{4,3,2,1,0:T(8,128)(2,1)} fusion(bf16[25,4,8,16,64]{4,2,3,1,0:T(8,128)(2,1)} %get-tuple-element.475, s32[1024]{0:T(1024)S(1)} %pad_clamp_fusion.2), kind=kCustom, calls=%fused_computation.clone.clone.1 | custom fusion | bytes 3276864 | tf_op jit(solution)/shard_map/while/body/eval_jaxpr/jit(_take)/gather | solution.py:145
  250.8 4.2 %fusion.148 = (f32[4,2,64]{2,1,0:T(2,128)S(1)}, f32[4,2,64,8,64]{2,4,3,1,0:T(8,128)S(1)}, f32[4,2,64,8,64,1]{2,4,5,3,1,0:T(8,128)S(1)}) fusion(f32[4,2,64]{2,1,0:T(2,128)S(1)} %fusion.146, f32[4,2,64]{2,1,0:T(2,128)S(1)} %get-tuple-element.425, f32[2,64,8,64]{1,3,2,0:T(8,128)S(1)} %copy.316, f32[4]{0:T(128)S(1)} %get-tuple-element.479, ...), kind=kOutput, calls=%fused_computation.14.clone.1 | convolution fusion | flops 108035584 | bytes 5257264 | tf_op jit(solution)/shard_map/while/body/eval_jaxpr/khdgi,khdgsj->hgisj/dot_general | solution.py:178
  256.9 2.2 fusion.150
  260.6 21.0 %dynamic_update_slice.22 = bf16[25,4,8,8,64]{4,3,2,1,0:T(8,128)(2,1)} dynamic-update-slice(bf16[25,4,8,8,64]{4,3,2,1,0:T(8,128)(2,1)} %get-tuple-element.452, bf16[25,4,8,2,64]{4,3,2,1,0:T(2,128)(2,1)S(1)} %copy.318, s32[]{:T(128)} %constant.183.clone.1..sunk, s32[]{:T(128)} %constant.183.clone.1..sunk, s32[]{:T(128)} %constant.183.clone.1..sunk, s32[]{:T(128)S(6)} %select_n.168, ...) | dynamic-update-slice | bytes 409604 | tf_op jit(solution)/shard_map/while/body/eval_jaxpr/dynamic_update_slice | solution.py:191
  292.7 1.9 constant_dynamic-slice_fusion.13
  295.6 5.3 %gather_fusion.2 = bf16[16,25,4,8,64]{4,3,2,1,0:T(8,128)(2,1)} fusion(bf16[25,4,8,16,64]{4,2,3,1,0:T(8,128)(2,1)} %get-tuple-element.475, s32[1024]{0:T(1024)S(1)} %pad_clamp_fusion.2), kind=kCustom, calls=%fused_computation.clone.clone.1 | custom fusion | bytes 3276864 | tf_op jit(solution)/shard_map/while/body/eval_jaxpr/jit(_take)/gather | solution.py:145
  300.8 4.2 %fusion.148 = (f32[4,2,64]{2,1,0:T(2,128)S(1)}, f32[4,2,64,8,64]{2,4,3,1,0:T(8,128)S(1)}, f32[4,2,64,8,64,1]{2,4,5,3,1,0:T(8,128)S(1)}) fusion(f32[4,2,64]{2,1,0:T(2,128)S(1)} %fusion.146, f32[4,2,64]{2,1,0:T(2,128)S(1)} %get-tuple-element.425, f32[2,64,8,64]{1,3,2,0:T(8,128)S(1)} %copy.316, f32[4]{0:T(128)S(1)} %get-tuple-element.479, ...), kind=kOutput, calls=%fused_computation.14.clone.1 | convolution fusion | flops 108035584 | bytes 5257264 | tf_op jit(solution)/shard_map/while/body/eval_jaxpr/khdgi,khdgsj->hgisj/dot_general | solution.py:178
  307.0 2.2 fusion.150
  310.7 21.0 %dynamic_update_slice.22 = bf16[25,4,8,8,64]{4,3,2,1,0:T(8,128)(2,1)} dynamic-update-slice(bf16[25,4,8,8,64]{4,3,2,1,0:T(8,128)(2,1)} %get-tuple-element.452, bf16[25,4,8,2,64]{4,3,2,1,0:T(2,128)(2,1)S(1)} %copy.318, s32[]{:T(128)} %constant.183.clone.1..sunk, s32[]{:T(128)} %constant.183.clone.1..sunk, s32[]{:T(128)} %constant.183.clone.1..sunk, s32[]{:T(128)S(6)} %select_n.168, ...) | dynamic-update-slice | bytes 409604 | tf_op jit(solution)/shard_map/while/body/eval_jaxpr/dynamic_update_slice | solution.py:191
  333.4 3.0 reshape.164
  336.5 6.5 %copy.221 = bf16[25,32,512]{1,0,2:T(8,128)(2,1)} copy(bf16[25,32,512]{2,1,0:T(8,128)(2,1)S(1)} %reshape.164) | data formatting | bytes 1638400 | tf_op jit(solution)/shard_map/reshape | solution.py:204
  343.0 5.3 %reshape.230 = bf16[4,2,51200]{2,1,0:T(2,128)(2,1)} reshape(bf16[512,25,32]{2,1,0:T(8,128)(2,1)} %bitcast.293) | data formatting | bytes 1638400
  348.3 5.2 %all-to-all-start.2 = ((bf16[4,2,51200]{2,1,0:T(2,128)(2,1)}), bf16[4,2,51200]{2,1,0:T(2,128)(2,1)S(1)}, u32[]{:S(2)}, u32[]{:S(2)}) async-start(bf16[4,2,51200]{2,1,0:T(2,128)(2,1)} %reshape.230), calls=%async_computation.2 | async-start | bytes 1638400 | tf_op jit(solution)/shard_map/all_to_all | solution.py:270
  354.2 2.5 collective-permute-start.7
  358.0 2.6 collective-permute-done.8
  363.2 19.1 %reduce-scatter.4.cloned.1.call-done = f32[128,3]{1,0:T(8,128)} async-done(((f32[512,3]{1,0:T(8,128)}), f32[128,3]{1,0:T(8,128)}) %reduce-scatter.4.cloned.1.call-update) | async-done | bytes 1552
  383.7 4.2 %reshape.231 = bf16[512,25,32]{2,1,0:T(8,128)(2,1)} reshape(bf16[4,2,51200]{2,1,0:T(2,128)(2,1)S(1)} %all-to-all-done.2) | data formatting | bytes 1638400
  387.9 5.2 %copy.244 = bf16[25,32,4,128]{3,2,1,0:T(4,128)(2,1)S(1)} copy(bf16[25,32,4,128]{1,0,3,2:T(8,128)(2,1)} %bitcast.294) | data formatting | bytes 1638400 | tf_op jit(solution)/shard_map/all_to_all | solution.py:270
  (250 shorter events, 92.2 us)
Async XLA Ops:
  7.2 16.6 %copy-start = (bf16[128,2048]{1,0:T(8,128)(2,1)S(1)}, bf16[128,2048]{1,0:T(8,128)(2,1)}, u32[]{:S(2)}) copy-start(bf16[128,2048]{1,0:T(8,128)(2,1)} %param.20) | copy-start | bytes 1572868
  16.7 12.9 %copy-start.9 = (f32[3,512]{1,0:T(4,128)S(1)}, f32[3,512]{1,0:T(4,128)}, u32[]{:S(2)}) copy-start(f32[3,512]{1,0:T(4,128)} %param.18) | copy-start | bytes 18436
  16.7 15.6 %copy-start.7 = (bf16[5,128,128]{2,1,0:T(8,128)(2,1)S(1)}, bf16[5,128,128]{2,1,0:T(8,128)(2,1)}, u32[]{:S(2)}) copy-start(bf16[5,128,128]{2,1,0:T(8,128)(2,1)} %param.22) | copy-start | bytes 491524
  16.8 56.8 %collective-permute-start = (bf16[1,25,32,128]{3,0,2,1:T(2,128)(2,1)}, bf16[1,25,32,128]{3,0,2,1:T(2,128)(2,1)}, u32[]{:S(2)}, u32[]{:S(2)}) collective-permute-start(bf16[1,25,32,128]{3,0,2,1:T(2,128)(2,1)} %get-tuple-element.311), channel_id=1, source_target_pairs={{0,1},{1,2},{2,3},{3,0},{4,5},{5,6},{6,7},{7,4},{8,9},{9,10},{10,1... | collective-permute-start | bytes 614408 | tf_op jit(solution)/shard_map/ppermute | solution.py:38
  19.8 63.9 %collective-permute-start.1 = (bf16[1,25,32,128]{3,0,2,1:T(2,128)(2,1)}, bf16[1,25,32,128]{3,0,2,1:T(2,128)(2,1)}, u32[]{:S(2)}, u32[]{:S(2)}) collective-permute-start(bf16[1,25,32,128]{3,0,2,1:T(2,128)(2,1)} %get-tuple-element.310), channel_id=1, source_target_pairs={{0,2},{1,3},{2,0},{3,1},{4,6},{5,7},{6,4},{7,5},{8,10},{9,11},{10,... | collective-permute-start | bytes 614408 | tf_op jit(solution)/shard_map/ppermute | solution.py:38
  22.4 71.5 %collective-permute-start.2 = (bf16[1,25,32,128]{3,0,2,1:T(2,128)(2,1)}, bf16[1,25,32,128]{3,0,2,1:T(2,128)(2,1)}, u32[]{:S(2)}, u32[]{:S(2)}) collective-permute-start(bf16[1,25,32,128]{3,0,2,1:T(2,128)(2,1)} %get-tuple-element.309), channel_id=1, source_target_pairs={{0,3},{1,0},{2,1},{3,2},{4,7},{5,4},{6,5},{7,6},{8,11},{9,8},{10,9... | collective-permute-start | bytes 614408 | tf_op jit(solution)/shard_map/ppermute | solution.py:38
  26.2 43.0 %all-to-all-start = ((bf16[2,1024,128]{2,0,1:T(2,128)(2,1)}), bf16[2,1024,128]{2,0,1:T(2,128)(2,1)S(1)}, u32[]{:S(2)}, u32[]{:S(2)}) async-start(bf16[2,1024,128]{2,0,1:T(2,128)(2,1)} %copy.194), calls=%async_computation | async-start | bytes 1048576 | tf_op jit(solution)/shard_map/all_to_all | solution.py:240
  29.7 9.9 %copy-start.6 = (f32[64,25,25]{0,2,1:T(8,128)S(1)}, f32[64,25,25]{0,2,1:T(8,128)}, u32[]{:S(2)}) copy-start(f32[64,25,25]{0,2,1:T(8,128)} %param.23) | copy-start | bytes 480004
  29.7 81.3 %collective-permute-start.5 = (f32[3,256]{1,0:T(4,128)S(1)}, f32[3,256]{1,0:T(4,128)S(1)}, u32[]{:S(2)}, u32[]{:S(2)}) collective-permute-start(f32[3,256]{1,0:T(4,128)S(1)} %get-tuple-element.316), channel_id=1, source_target_pairs={{0,4},{4,8},{8,12},{12,16},{16,20},{20,24},{24,28},{28,0},{1,5},{5... | collective-permute-start | bytes 9224 | tf_op jit(solution)/shard_map/ppermute | solution.py:52
  29.8 81.2 %collective-permute-start.6 = (f32[3,256]{1,0:T(4,128)S(1)}, f32[3,256]{1,0:T(4,128)S(1)}, u32[]{:S(2)}, u32[]{:S(2)}) collective-permute-start(f32[3,256]{1,0:T(4,128)S(1)} %get-tuple-element.317), channel_id=1, source_target_pairs={{4,0},{8,4},{12,8},{16,12},{20,16},{24,20},{28,24},{0,28},{5,1},{9... | collective-permute-start | bytes 9224 | tf_op jit(solution)/shard_map/ppermute | solution.py:53
  42.5 31.0 %copy-start.10 = (s32[8,8]{1,0:T(8,128)S(1)}, s32[8,8]{1,0:T(8,128)}, u32[]{:S(2)}) copy-start(s32[8,8]{1,0:T(8,128)} %param.25) | copy-start | bytes 772
  69.2 43.2 %all-to-all-start.1 = ((bf16[25,128,128]{2,0,1:T(8,128)(2,1)}), bf16[25,128,128]{2,0,1:T(8,128)(2,1)}, u32[]{:S(2)}, u32[]{:S(2)}) async-start(bf16[25,128,128]{2,0,1:T(8,128)(2,1)} %copy.212), calls=%async_computation.1 | async-start | bytes 2097152 | tf_op jit(solution)/shard_map/all_to_all | solution.py:242
  104.3 4.1 %copy-start.12 = (s32[8]{0:T(128)S(1)}, s32[8]{0:T(128)}, u32[]{:S(2)}) copy-start(s32[8]{0:T(128)} %param.26) | copy-start | bytes 100
  104.6 4.6 %copy-start.11 = (s32[8]{0:T(128)S(1)}, s32[8]{0:T(128)}, u32[]{:S(2)}) copy-start(s32[8]{0:T(128)} %param.24) | copy-start | bytes 100
  105.7 5.2 %copy-start.13 = (f32[16]{0:T(128)S(1)}, f32[16]{0:T(128)}, u32[]{:S(2)}) copy-start(f32[16]{0:T(128)} %param.19) | copy-start | bytes 196
  105.7 13.9 %collective-permute-start.3 = (bf16[1056,256]{1,0:T(8,128)(2,1)}, bf16[1056,256]{1,0:T(8,128)(2,1)}, u32[]{:S(2)}, u32[]{:S(2)}) collective-permute-start(bf16[1056,256]{1,0:T(8,128)(2,1)} %get-tuple-element.307), channel_id=1, source_target_pairs={{0,4},{4,8},{8,12},{12,16},{16,20},{20,24},{24,28},{28,0},{1,5},{5... | collective-permute-start | bytes 1622024 | tf_op jit(solution)/shard_map/ppermute | solution.py:52
  105.7 13.9 %collective-permute-start.4 = (bf16[1056,256]{1,0:T(8,128)(2,1)}, bf16[1056,256]{1,0:T(8,128)(2,1)}, u32[]{:S(2)}, u32[]{:S(2)}) collective-permute-start(bf16[1056,256]{1,0:T(8,128)(2,1)} %get-tuple-element.308), channel_id=1, source_target_pairs={{4,0},{8,4},{12,8},{16,12},{20,16},{24,20},{28,24},{0,28},{5,1},{9... | collective-permute-start | bytes 1622024 | tf_op jit(solution)/shard_map/ppermute | solution.py:53
  133.4 4.9 %copy-start.3 = (bf16[4,64,16,64]{3,1,2,0:T(8,128)(2,1)}, bf16[4,64,16,64]{3,1,2,0:T(8,128)(2,1)S(1)}, u32[]{:S(2)}) copy-start(bf16[4,64,16,64]{3,1,2,0:T(8,128)(2,1)S(1)} %get-tuple-element.478) | copy-start | bytes 1572868 | tf_op jit(solution)/shard_map/while
  155.0 1.9 copy-start.2
  160.2 23.2 %copy-start.4 = (bf16[4,64,16,64]{3,1,2,0:T(8,128)(2,1)S(1)}, bf16[4,64,16,64]{3,1,2,0:T(8,128)(2,1)}, u32[]{:S(2)}) copy-start(bf16[4,64,16,64]{3,1,2,0:T(8,128)(2,1)} %copy-done.3) | copy-start | bytes 1572868 | tf_op jit(solution)/shard_map/while
  183.4 4.9 %copy-start.3 = (bf16[4,64,16,64]{3,1,2,0:T(8,128)(2,1)}, bf16[4,64,16,64]{3,1,2,0:T(8,128)(2,1)S(1)}, u32[]{:S(2)}) copy-start(bf16[4,64,16,64]{3,1,2,0:T(8,128)(2,1)S(1)} %get-tuple-element.478) | copy-start | bytes 1572868 | tf_op jit(solution)/shard_map/while
  205.0 1.9 copy-start.2
  210.2 23.2 %copy-start.4 = (bf16[4,64,16,64]{3,1,2,0:T(8,128)(2,1)S(1)}, bf16[4,64,16,64]{3,1,2,0:T(8,128)(2,1)}, u32[]{:S(2)}) copy-start(bf16[4,64,16,64]{3,1,2,0:T(8,128)(2,1)} %copy-done.3) | copy-start | bytes 1572868 | tf_op jit(solution)/shard_map/while
  233.4 4.9 %copy-start.3 = (bf16[4,64,16,64]{3,1,2,0:T(8,128)(2,1)}, bf16[4,64,16,64]{3,1,2,0:T(8,128)(2,1)S(1)}, u32[]{:S(2)}) copy-start(bf16[4,64,16,64]{3,1,2,0:T(8,128)(2,1)S(1)} %get-tuple-element.478) | copy-start | bytes 1572868 | tf_op jit(solution)/shard_map/while
  255.0 1.9 copy-start.2
  260.2 23.2 %copy-start.4 = (bf16[4,64,16,64]{3,1,2,0:T(8,128)(2,1)S(1)}, bf16[4,64,16,64]{3,1,2,0:T(8,128)(2,1)}, u32[]{:S(2)}) copy-start(bf16[4,64,16,64]{3,1,2,0:T(8,128)(2,1)} %copy-done.3) | copy-start | bytes 1572868 | tf_op jit(solution)/shard_map/while
  283.4 4.9 %copy-start.3 = (bf16[4,64,16,64]{3,1,2,0:T(8,128)(2,1)}, bf16[4,64,16,64]{3,1,2,0:T(8,128)(2,1)S(1)}, u32[]{:S(2)}) copy-start(bf16[4,64,16,64]{3,1,2,0:T(8,128)(2,1)S(1)} %get-tuple-element.478) | copy-start | bytes 1572868 | tf_op jit(solution)/shard_map/while
  305.0 1.9 copy-start.2
  310.2 23.2 %copy-start.4 = (bf16[4,64,16,64]{3,1,2,0:T(8,128)(2,1)S(1)}, bf16[4,64,16,64]{3,1,2,0:T(8,128)(2,1)}, u32[]{:S(2)}) copy-start(bf16[4,64,16,64]{3,1,2,0:T(8,128)(2,1)} %copy-done.3) | copy-start | bytes 1572868 | tf_op jit(solution)/shard_map/while
  348.3 13.9 %copy-start.5 = (bf16[25,128,128]{2,1,0:T(8,128)(2,1)S(1)}, bf16[25,128,128]{2,1,0:T(8,128)(2,1)}, u32[]{:S(2)}) copy-start(bf16[25,128,128]{2,1,0:T(8,128)(2,1)} %param.17) | copy-start | bytes 2457604
  348.3 35.5 %all-to-all-start.2 = ((bf16[4,2,51200]{2,1,0:T(2,128)(2,1)}), bf16[4,2,51200]{2,1,0:T(2,128)(2,1)S(1)}, u32[]{:S(2)}, u32[]{:S(2)}) async-start(bf16[4,2,51200]{2,1,0:T(2,128)(2,1)} %reshape.230), calls=%async_computation.2 | async-start | bytes 1638400 | tf_op jit(solution)/shard_map/all_to_all | solution.py:270
  353.4 28.8 %reduce-scatter.4.cloned.1.call-start = ((), (), s32[]{:S(2)}) async-start(), calls=%async_computation.4 | async-start | bytes 327680
  354.2 3.8 collective-permute-start.7
  356.7 3.9 collective-permute-start.8
  387.9 5.6 %copy-start.8 = (bf16[5,128,128]{2,1,0:T(8,128)(2,1)S(1)}, bf16[5,128,128]{2,1,0:T(8,128)(2,1)}, u32[]{:S(2)}) copy-start(bf16[5,128,128]{2,1,0:T(8,128)(2,1)} %param.22) | copy-start | bytes 491524
  394.6 2.0 copy-start.1
Sparse Core Ops, SparseCore 0:
  362.3 19.9 reduce-scatter.3
